TPU v7x, 512 devices: a whole 4x8x8 slice. The times are simulated.
512 devices in a mesh: tm: 32 (over y, x), blk: 16 (over z, core).
Axes of the slice: x: 4, y: 8, z: 8, core: 2. Of those that a mesh axis runs over, the one named last changes fastest.
Arguments:
- panel_strip: bfloat16 [32, 8192, 2304], P('tm', 'blk'), may hold values from -6 to 6
- pivot_inverses: bfloat16 [32, 2, 256, 256], P('tm'), may hold values from -0.0234375 to 0.0234375
- coupling: float32 [32, 256, 256], P('tm'), may hold values from -0.375 to 0.375
- pivot_nodes: int32 [3, 256], replicated, may hold values from 0 to 8191, as said below
Outputs:
- trailing: bfloat16 [32, 8192, 1792], P('tm', 'blk')
- reduced: float32 [32, 256, 256], P('tm')
Inputs may be any that keep to these rules, and one draw needn't show every extreme that they name: `pivot_nodes`: entry j of every row is a node of the range [(j // 16) * 512, (j // 16 + 1) * 512); all 768 entries differ.
All inputs are finite; a program needn't handle non-finite values.
Results may differ from a plain program's by a relative error of at most 0.0068.
Values may be sent and summed in bfloat16 or wider, within the bound.
No kernel may reach another device: no remote copies, remote signals or barrier semaphores. Data moves between devices by JAX's collectives and lax.ppermute only.
A program may use at most 128 MiB of HBM per device.

v0:
```python
import jax
import jax.numpy as jnp
from jax import lax
from jax.sharding import PartitionSpec as P


def passed_along(x, axis, by):
    count = lax.axis_size(axis)
    pairs = [(i, i + by) for i in range(count) if 0 <= i + by < count]
    return lax.ppermute(x, axis, pairs)


def matmul_high(left, right):
    return jnp.dot(left, right, precision=lax.Precision.HIGHEST, preferred_element_type=jnp.float32)


def body(panel_strip, pivot_inverses, coupling, pivot_nodes):
    strip_block = panel_strip[0]
    inverse_pair = pivot_inverses[0]
    coupling_here = coupling[0]
    panel_width = inverse_pair.shape[-1]
    rows_here = strip_block.shape[0]
    blk_count = lax.axis_size("blk")
    per_device = panel_width // blk_count
    my_index = lax.axis_index("blk")
    local_rows = (
        lax.dynamic_slice_in_dim(pivot_nodes, my_index * per_device, per_device, 1)
        - my_index * rows_here
    )
    picker = (
        local_rows[:, :, None] == lax.broadcasted_iota(jnp.int32, (3, per_device, rows_here), 2)
    ).astype(jnp.bfloat16)
    factor_one = jnp.dot(
        strip_block[:, :panel_width], inverse_pair[0], preferred_element_type=jnp.float32
    ).astype(jnp.bfloat16)
    picked_one = jnp.dot(
        picker[0], strip_block[:, panel_width:], preferred_element_type=jnp.float32
    ).astype(jnp.bfloat16)
    columns = factor_one
    updated = (
        strip_block[:, panel_width:].astype(jnp.float32)
        - jnp.dot(
            columns,
            lax.all_gather(picked_one, "blk", axis=0, tiled=True),
            preferred_element_type=jnp.float32,
        )
    ).astype(jnp.bfloat16)
    factor_two = jnp.dot(
        updated[:, :panel_width], inverse_pair[1], preferred_element_type=jnp.float32
    ).astype(jnp.bfloat16)
    picked_two = jnp.dot(
        picker[1], updated[:, panel_width:], preferred_element_type=jnp.float32
    ).astype(jnp.bfloat16)
    columns = factor_two
    trailing = (
        updated[:, panel_width:].astype(jnp.float32)
        - jnp.dot(
            columns,
            lax.all_gather(picked_two, "blk", axis=0, tiled=True),
            preferred_element_type=jnp.float32,
        )
    ).astype(jnp.bfloat16)
    edge_rows = jnp.dot(
        picker[2], trailing[:, :panel_width], preferred_element_type=jnp.float32
    ).astype(jnp.bfloat16)
    boundary_block = lax.all_gather(edge_rows, "blk", axis=0, tiled=True).astype(jnp.float32)
    position = lax.axis_index("tm")

    def advance(turn_index, current):
        incoming = passed_along(current, "tm", 1)

        def apply_map(operand):
            return (
                matmul_high(matmul_high(coupling_here, operand), coupling_here.T) + boundary_block
            )

        def keep_state(operand):
            return current

        return lax.cond(position == turn_index, apply_map, keep_state, incoming)

    reduced = lax.fori_loop(1, lax.axis_size("tm"), advance, boundary_block)
    return (trailing[None], reduced[None])


def solution(mesh):
    placed = (P("tm", "blk", None), P("tm", None, None, None), P("tm", None, None), P())
    return jax.shard_map(
        body,
        mesh=mesh,
        in_specs=placed,
        out_specs=(P("tm", "blk", None), P("tm", None, None)),
        check_vma=False,
    )
```

profile of v0, /device:TPU:32, one launch (start us, length us, event | category | flops | bytes accessed | tf_op | source)
XLA Modules:
  0.0 484.5 jit_solution(10073837723274590851)
XLA Ops:
  8.1 2.6 convolution_convert_fusion.1
  10.7 46.4 %all-gather.2.cloned.1.call-done = bf16[256,2048]{1,0:T(8,128)(2,1)} async-done(((bf16[16,2048]{1,0:T(8,128)(2,1)}), bf16[256,2048]{1,0:T(8,128)(2,1)}) %all-gather.2.cloned.1.call-update) | async-done | bytes 1048592 | tf_op jit(solution)/shard_map/all_gather | solution.py:44
  57.1 2.8 subtract_convert_fusion
  60.3 18.0 %all_gather.10 = bf16[256,1792]{1,0:T(8,128)(2,1)S(1)} all-gather(bf16[16,1792]{1,0:T(8,128)(2,1)S(1)} %convolution_convert_fusion), channel_id=1, replica_groups=mesh['tm'=32,'blk'=16] {'blk'}, dimensions={0}, use_global_device_ids=true | all-gather | bytes 974848 | tf_op jit(solution)/shard_map/all_gather | solution.py:59
  78.3 3.0 subtract_convert_fusion.1
  82.4 15.1 %all_gather.11 = bf16[256,256]{1,0:T(8,128)(2,1)S(1)} all-gather(bf16[16,256]{1,0:T(8,128)(2,1)S(1)} %convolution_convert_fusion.4), channel_id=1, replica_groups=mesh['tm'=32,'blk'=16] {'blk'}, dimensions={0}, use_global_device_ids=true | all-gather | bytes 139264 | tf_op jit(solution)/shard_map/all_gather | solution.py:66
  97.6 379.3 %while.16 = (s32[]{:T(128)}, f32[256,256]{1,0:T(8,128)S(1)}, s32[]{:T(128)}, f32[256,256]{1,0:T(8,128)S(1)}, f32[256,256]{1,0:T(8,128)S(1)}, /*index=5*/s32[]{:T(128)}) while((s32[]{:T(128)}, f32[256,256]{1,0:T(8,128)S(1)}, s32[]{:T(128)}, f32[256,256]{1,0:T(8,128)S(1)}, f32[256,256]{1,0:T(8,128)S(1)}, /*index=5*/s32[]{:T(128)}) %tuple.51), condition=%wide.region_3.0_spmd, body=%wide.region_0.0_spmd.sunk | while | flops 402718720 | bytes 2883739 | solution.py:82
  97.6 3.4 collective-permute-start
  101.0 10.4 %collective-permute-done = f32[256,256]{1,0:T(8,128)S(1)} collective-permute-done((f32[256,256]{1,0:T(8,128)S(1)}, f32[256,256]{1,0:T(8,128)S(1)}, u32[]{:S(2)}, u32[]{:S(2)}) %collective-permute-start) | collective-permute-done | bytes 262176 | tf_op jit(solution)/shard_map/while/body/eval_jaxpr/ppermute | solution.py:10
  111.4 1.9 collective-permute-start
  113.3 11.0 %collective-permute-done = f32[256,256]{1,0:T(8,128)S(1)} collective-permute-done((f32[256,256]{1,0:T(8,128)S(1)}, f32[256,256]{1,0:T(8,128)S(1)}, u32[]{:S(2)}, u32[]{:S(2)}) %collective-permute-start) | collective-permute-done | bytes 262176 | tf_op jit(solution)/shard_map/while/body/eval_jaxpr/ppermute | solution.py:10
  124.3 1.9 collective-permute-start
  126.3 10.1 %collective-permute-done = f32[256,256]{1,0:T(8,128)S(1)} collective-permute-done((f32[256,256]{1,0:T(8,128)S(1)}, f32[256,256]{1,0:T(8,128)S(1)}, u32[]{:S(2)}, u32[]{:S(2)}) %collective-permute-start) | collective-permute-done | bytes 262176 | tf_op jit(solution)/shard_map/while/body/eval_jaxpr/ppermute | solution.py:10
  136.4 1.9 collective-permute-start
  138.3 9.7 %collective-permute-done = f32[256,256]{1,0:T(8,128)S(1)} collective-permute-done((f32[256,256]{1,0:T(8,128)S(1)}, f32[256,256]{1,0:T(8,128)S(1)}, u32[]{:S(2)}, u32[]{:S(2)}) %collective-permute-start) | collective-permute-done | bytes 262176 | tf_op jit(solution)/shard_map/while/body/eval_jaxpr/ppermute | solution.py:10
  147.9 1.9 collective-permute-start
  149.9 9.7 %collective-permute-done = f32[256,256]{1,0:T(8,128)S(1)} collective-permute-done((f32[256,256]{1,0:T(8,128)S(1)}, f32[256,256]{1,0:T(8,128)S(1)}, u32[]{:S(2)}, u32[]{:S(2)}) %collective-permute-start) | collective-permute-done | bytes 262176 | tf_op jit(solution)/shard_map/while/body/eval_jaxpr/ppermute | solution.py:10
  159.5 1.9 collective-permute-start
  161.4 9.7 %collective-permute-done = f32[256,256]{1,0:T(8,128)S(1)} collective-permute-done((f32[256,256]{1,0:T(8,128)S(1)}, f32[256,256]{1,0:T(8,128)S(1)}, u32[]{:S(2)}, u32[]{:S(2)}) %collective-permute-start) | collective-permute-done | bytes 262176 | tf_op jit(solution)/shard_map/while/body/eval_jaxpr/ppermute | solution.py:10
  171.1 1.9 collective-permute-start
  173.0 9.7 %collective-permute-done = f32[256,256]{1,0:T(8,128)S(1)} collective-permute-done((f32[256,256]{1,0:T(8,128)S(1)}, f32[256,256]{1,0:T(8,128)S(1)}, u32[]{:S(2)}, u32[]{:S(2)}) %collective-permute-start) | collective-permute-done | bytes 262176 | tf_op jit(solution)/shard_map/while/body/eval_jaxpr/ppermute | solution.py:10
  182.7 1.9 collective-permute-start
  184.6 9.8 %collective-permute-done = f32[256,256]{1,0:T(8,128)S(1)} collective-permute-done((f32[256,256]{1,0:T(8,128)S(1)}, f32[256,256]{1,0:T(8,128)S(1)}, u32[]{:S(2)}, u32[]{:S(2)}) %collective-permute-start) | collective-permute-done | bytes 262176 | tf_op jit(solution)/shard_map/while/body/eval_jaxpr/ppermute | solution.py:10
  194.4 1.9 collective-permute-start
  196.3 10.9 %collective-permute-done = f32[256,256]{1,0:T(8,128)S(1)} collective-permute-done((f32[256,256]{1,0:T(8,128)S(1)}, f32[256,256]{1,0:T(8,128)S(1)}, u32[]{:S(2)}, u32[]{:S(2)}) %collective-permute-start) | collective-permute-done | bytes 262176 | tf_op jit(solution)/shard_map/while/body/eval_jaxpr/ppermute | solution.py:10
  209.2 12.1 %collective-permute-done = f32[256,256]{1,0:T(8,128)S(1)} collective-permute-done((f32[256,256]{1,0:T(8,128)S(1)}, f32[256,256]{1,0:T(8,128)S(1)}, u32[]{:S(2)}, u32[]{:S(2)}) %collective-permute-start) | collective-permute-done | bytes 262176 | tf_op jit(solution)/shard_map/while/body/eval_jaxpr/ppermute | solution.py:10
  223.3 11.6 %collective-permute-done = f32[256,256]{1,0:T(8,128)S(1)} collective-permute-done((f32[256,256]{1,0:T(8,128)S(1)}, f32[256,256]{1,0:T(8,128)S(1)}, u32[]{:S(2)}, u32[]{:S(2)}) %collective-permute-start) | collective-permute-done | bytes 262176 | tf_op jit(solution)/shard_map/while/body/eval_jaxpr/ppermute | solution.py:10
  236.8 10.8 %collective-permute-done = f32[256,256]{1,0:T(8,128)S(1)} collective-permute-done((f32[256,256]{1,0:T(8,128)S(1)}, f32[256,256]{1,0:T(8,128)S(1)}, u32[]{:S(2)}, u32[]{:S(2)}) %collective-permute-start) | collective-permute-done | bytes 262176 | tf_op jit(solution)/shard_map/while/body/eval_jaxpr/ppermute | solution.py:10
  249.5 9.9 %collective-permute-done = f32[256,256]{1,0:T(8,128)S(1)} collective-permute-done((f32[256,256]{1,0:T(8,128)S(1)}, f32[256,256]{1,0:T(8,128)S(1)}, u32[]{:S(2)}, u32[]{:S(2)}) %collective-permute-start) | collective-permute-done | bytes 262176 | tf_op jit(solution)/shard_map/while/body/eval_jaxpr/ppermute | solution.py:10
  261.3 9.7 %collective-permute-done = f32[256,256]{1,0:T(8,128)S(1)} collective-permute-done((f32[256,256]{1,0:T(8,128)S(1)}, f32[256,256]{1,0:T(8,128)S(1)}, u32[]{:S(2)}, u32[]{:S(2)}) %collective-permute-start) | collective-permute-done | bytes 262176 | tf_op jit(solution)/shard_map/while/body/eval_jaxpr/ppermute | solution.py:10
  272.9 9.7 %collective-permute-done = f32[256,256]{1,0:T(8,128)S(1)} collective-permute-done((f32[256,256]{1,0:T(8,128)S(1)}, f32[256,256]{1,0:T(8,128)S(1)}, u32[]{:S(2)}, u32[]{:S(2)}) %collective-permute-start) | collective-permute-done | bytes 262176 | tf_op jit(solution)/shard_map/while/body/eval_jaxpr/ppermute | solution.py:10
  284.5 9.7 %collective-permute-done = f32[256,256]{1,0:T(8,128)S(1)} collective-permute-done((f32[256,256]{1,0:T(8,128)S(1)}, f32[256,256]{1,0:T(8,128)S(1)}, u32[]{:S(2)}, u32[]{:S(2)}) %collective-permute-start) | collective-permute-done | bytes 262176 | tf_op jit(solution)/shard_map/while/body/eval_jaxpr/ppermute | solution.py:10
  294.9 1.9 collective-permute-start
  296.9 9.7 %collective-permute-done = f32[256,256]{1,0:T(8,128)S(1)} collective-permute-done((f32[256,256]{1,0:T(8,128)S(1)}, f32[256,256]{1,0:T(8,128)S(1)}, u32[]{:S(2)}, u32[]{:S(2)}) %collective-permute-start) | collective-permute-done | bytes 262176 | tf_op jit(solution)/shard_map/while/body/eval_jaxpr/ppermute | solution.py:10
  308.4 10.1 %collective-permute-done = f32[256,256]{1,0:T(8,128)S(1)} collective-permute-done((f32[256,256]{1,0:T(8,128)S(1)}, f32[256,256]{1,0:T(8,128)S(1)}, u32[]{:S(2)}, u32[]{:S(2)}) %collective-permute-start) | collective-permute-done | bytes 262176 | tf_op jit(solution)/shard_map/while/body/eval_jaxpr/ppermute | solution.py:10
  320.4 11.2 %collective-permute-done = f32[256,256]{1,0:T(8,128)S(1)} collective-permute-done((f32[256,256]{1,0:T(8,128)S(1)}, f32[256,256]{1,0:T(8,128)S(1)}, u32[]{:S(2)}, u32[]{:S(2)}) %collective-permute-start) | collective-permute-done | bytes 262176 | tf_op jit(solution)/shard_map/while/body/eval_jaxpr/ppermute | solution.py:10
  333.6 12.3 %collective-permute-done = f32[256,256]{1,0:T(8,128)S(1)} collective-permute-done((f32[256,256]{1,0:T(8,128)S(1)}, f32[256,256]{1,0:T(8,128)S(1)}, u32[]{:S(2)}, u32[]{:S(2)}) %collective-permute-start) | collective-permute-done | bytes 262176 | tf_op jit(solution)/shard_map/while/body/eval_jaxpr/ppermute | solution.py:10
  347.8 11.6 %collective-permute-done = f32[256,256]{1,0:T(8,128)S(1)} collective-permute-done((f32[256,256]{1,0:T(8,128)S(1)}, f32[256,256]{1,0:T(8,128)S(1)}, u32[]{:S(2)}, u32[]{:S(2)}) %collective-permute-start) | collective-permute-done | bytes 262176 | tf_op jit(solution)/shard_map/while/body/eval_jaxpr/ppermute | solution.py:10
  361.3 10.8 %collective-permute-done = f32[256,256]{1,0:T(8,128)S(1)} collective-permute-done((f32[256,256]{1,0:T(8,128)S(1)}, f32[256,256]{1,0:T(8,128)S(1)}, u32[]{:S(2)}, u32[]{:S(2)}) %collective-permute-start) | collective-permute-done | bytes 262176 | tf_op jit(solution)/shard_map/while/body/eval_jaxpr/ppermute | solution.py:10
  374.0 9.8 %collective-permute-done = f32[256,256]{1,0:T(8,128)S(1)} collective-permute-done((f32[256,256]{1,0:T(8,128)S(1)}, f32[256,256]{1,0:T(8,128)S(1)}, u32[]{:S(2)}, u32[]{:S(2)}) %collective-permute-start) | collective-permute-done | bytes 262176 | tf_op jit(solution)/shard_map/while/body/eval_jaxpr/ppermute | solution.py:10
  385.8 9.7 %collective-permute-done = f32[256,256]{1,0:T(8,128)S(1)} collective-permute-done((f32[256,256]{1,0:T(8,128)S(1)}, f32[256,256]{1,0:T(8,128)S(1)}, u32[]{:S(2)}, u32[]{:S(2)}) %collective-permute-start) | collective-permute-done | bytes 262176 | tf_op jit(solution)/shard_map/while/body/eval_jaxpr/ppermute | solution.py:10
  397.4 9.7 %collective-permute-done = f32[256,256]{1,0:T(8,128)S(1)} collective-permute-done((f32[256,256]{1,0:T(8,128)S(1)}, f32[256,256]{1,0:T(8,128)S(1)}, u32[]{:S(2)}, u32[]{:S(2)}) %collective-permute-start) | collective-permute-done | bytes 262176 | tf_op jit(solution)/shard_map/while/body/eval_jaxpr/ppermute | solution.py:10
  409.0 9.7 %collective-permute-done = f32[256,256]{1,0:T(8,128)S(1)} collective-permute-done((f32[256,256]{1,0:T(8,128)S(1)}, f32[256,256]{1,0:T(8,128)S(1)}, u32[]{:S(2)}, u32[]{:S(2)}) %collective-permute-start) | collective-permute-done | bytes 262176 | tf_op jit(solution)/shard_map/while/body/eval_jaxpr/ppermute | solution.py:10
  420.5 9.7 %collective-permute-done = f32[256,256]{1,0:T(8,128)S(1)} collective-permute-done((f32[256,256]{1,0:T(8,128)S(1)}, f32[256,256]{1,0:T(8,128)S(1)}, u32[]{:S(2)}, u32[]{:S(2)}) %collective-permute-start) | collective-permute-done | bytes 262176 | tf_op jit(solution)/shard_map/while/body/eval_jaxpr/ppermute | solution.py:10
  432.1 10.1 %collective-permute-done = f32[256,256]{1,0:T(8,128)S(1)} collective-permute-done((f32[256,256]{1,0:T(8,128)S(1)}, f32[256,256]{1,0:T(8,128)S(1)}, u32[]{:S(2)}, u32[]{:S(2)}) %collective-permute-start) | collective-permute-done | bytes 262176 | tf_op jit(solution)/shard_map/while/body/eval_jaxpr/ppermute | solution.py:10
  444.1 9.7 %collective-permute-done = f32[256,256]{1,0:T(8,128)S(1)} collective-permute-done((f32[256,256]{1,0:T(8,128)S(1)}, f32[256,256]{1,0:T(8,128)S(1)}, u32[]{:S(2)}, u32[]{:S(2)}) %collective-permute-start) | collective-permute-done | bytes 262176 | tf_op jit(solution)/shard_map/while/body/eval_jaxpr/ppermute | solution.py:10
  455.7 9.7 %collective-permute-done = f32[256,256]{1,0:T(8,128)S(1)} collective-permute-done((f32[256,256]{1,0:T(8,128)S(1)}, f32[256,256]{1,0:T(8,128)S(1)}, u32[]{:S(2)}, u32[]{:S(2)}) %collective-permute-start) | collective-permute-done | bytes 262176 | tf_op jit(solution)/shard_map/while/body/eval_jaxpr/ppermute | solution.py:10
  467.3 9.7 %collective-permute-done = f32[256,256]{1,0:T(8,128)S(1)} collective-permute-done((f32[256,256]{1,0:T(8,128)S(1)}, f32[256,256]{1,0:T(8,128)S(1)}, u32[]{:S(2)}, u32[]{:S(2)}) %collective-permute-start) | collective-permute-done | bytes 262176 | tf_op jit(solution)/shard_map/while/body/eval_jaxpr/ppermute | solution.py:10
  (68 shorter events, 44.8 us)
Async XLA Ops:
  7.2 50.0 %copy-start.2 = (bf16[1,2,256,256]{3,2,1,0:T(8,128)(2,1)S(1)}, bf16[1,2,256,256]{3,2,1,0:T(8,128)(2,1)}, u32[]{:S(2)}) copy-start(bf16[1,2,256,256]{3,2,1,0:T(8,128)(2,1)} %param.9) | copy-start | bytes 786436
  7.2 50.0 %all-gather.2.cloned.1.call-start = ((), (), s32[]{:S(2)}) async-start(), calls=%async_computation | async-start | bytes 1114112 | tf_op jit(solution)/shard_map/all_gather | solution.py:44
  78.3 19.3 %copy-start = (f32[1,256,256]{2,1,0:T(8,128)S(1)}, f32[1,256,256]{2,1,0:T(8,128)}, u32[]{:S(2)}) copy-start(f32[1,256,256]{2,1,0:T(8,128)} %param.10) | copy-start | bytes 786436
  97.6 13.8 %collective-permute-start = (f32[256,256]{1,0:T(8,128)S(1)}, f32[256,256]{1,0:T(8,128)S(1)}, u32[]{:S(2)}, u32[]{:S(2)}) collective-permute-start(f32[256,256]{1,0:T(8,128)S(1)} %get-tuple-element.162), channel_id=1, source_target_pairs={{0,16},{16,32},{32,48},{48,64},{64,80},{80,96},{96,112},{112,128},... | collective-permute-start | bytes 786440 | tf_op jit(solution)/shard_map/while/body/eval_jaxpr/ppermute | solution.py:10
  111.4 13.0 %collective-permute-start = (f32[256,256]{1,0:T(8,128)S(1)}, f32[256,256]{1,0:T(8,128)S(1)}, u32[]{:S(2)}, u32[]{:S(2)}) collective-permute-start(f32[256,256]{1,0:T(8,128)S(1)} %get-tuple-element.162), channel_id=1, source_target_pairs={{0,16},{16,32},{32,48},{48,64},{64,80},{80,96},{96,112},{112,128},... | collective-permute-start | bytes 786440 | tf_op jit(solution)/shard_map/while/body/eval_jaxpr/ppermute | solution.py:10
  124.3 12.0 %collective-permute-start = (f32[256,256]{1,0:T(8,128)S(1)}, f32[256,256]{1,0:T(8,128)S(1)}, u32[]{:S(2)}, u32[]{:S(2)}) collective-permute-start(f32[256,256]{1,0:T(8,128)S(1)} %get-tuple-element.162), channel_id=1, source_target_pairs={{0,16},{16,32},{32,48},{48,64},{64,80},{80,96},{96,112},{112,128},... | collective-permute-start | bytes 786440 | tf_op jit(solution)/shard_map/while/body/eval_jaxpr/ppermute | solution.py:10
  136.4 11.6 %collective-permute-start = (f32[256,256]{1,0:T(8,128)S(1)}, f32[256,256]{1,0:T(8,128)S(1)}, u32[]{:S(2)}, u32[]{:S(2)}) collective-permute-start(f32[256,256]{1,0:T(8,128)S(1)} %get-tuple-element.162), channel_id=1, source_target_pairs={{0,16},{16,32},{32,48},{48,64},{64,80},{80,96},{96,112},{112,128},... | collective-permute-start | bytes 786440 | tf_op jit(solution)/shard_map/while/body/eval_jaxpr/ppermute | solution.py:10
  147.9 11.6 %collective-permute-start = (f32[256,256]{1,0:T(8,128)S(1)}, f32[256,256]{1,0:T(8,128)S(1)}, u32[]{:S(2)}, u32[]{:S(2)}) collective-permute-start(f32[256,256]{1,0:T(8,128)S(1)} %get-tuple-element.162), channel_id=1, source_target_pairs={{0,16},{16,32},{32,48},{48,64},{64,80},{80,96},{96,112},{112,128},... | collective-permute-start | bytes 786440 | tf_op jit(solution)/shard_map/while/body/eval_jaxpr/ppermute | solution.py:10
  159.5 11.6 %collective-permute-start = (f32[256,256]{1,0:T(8,128)S(1)}, f32[256,256]{1,0:T(8,128)S(1)}, u32[]{:S(2)}, u32[]{:S(2)}) collective-permute-start(f32[256,256]{1,0:T(8,128)S(1)} %get-tuple-element.162), channel_id=1, source_target_pairs={{0,16},{16,32},{32,48},{48,64},{64,80},{80,96},{96,112},{112,128},... | collective-permute-start | bytes 786440 | tf_op jit(solution)/shard_map/while/body/eval_jaxpr/ppermute | solution.py:10
  171.1 11.6 %collective-permute-start = (f32[256,256]{1,0:T(8,128)S(1)}, f32[256,256]{1,0:T(8,128)S(1)}, u32[]{:S(2)}, u32[]{:S(2)}) collective-permute-start(f32[256,256]{1,0:T(8,128)S(1)} %get-tuple-element.162), channel_id=1, source_target_pairs={{0,16},{16,32},{32,48},{48,64},{64,80},{80,96},{96,112},{112,128},... | collective-permute-start | bytes 786440 | tf_op jit(solution)/shard_map/while/body/eval_jaxpr/ppermute | solution.py:10
  182.7 11.8 %collective-permute-start = (f32[256,256]{1,0:T(8,128)S(1)}, f32[256,256]{1,0:T(8,128)S(1)}, u32[]{:S(2)}, u32[]{:S(2)}) collective-permute-start(f32[256,256]{1,0:T(8,128)S(1)} %get-tuple-element.162), channel_id=1, source_target_pairs={{0,16},{16,32},{32,48},{48,64},{64,80},{80,96},{96,112},{112,128},... | collective-permute-start | bytes 786440 | tf_op jit(solution)/shard_map/while/body/eval_jaxpr/ppermute | solution.py:10
  194.4 12.8 %collective-permute-start = (f32[256,256]{1,0:T(8,128)S(1)}, f32[256,256]{1,0:T(8,128)S(1)}, u32[]{:S(2)}, u32[]{:S(2)}) collective-permute-start(f32[256,256]{1,0:T(8,128)S(1)} %get-tuple-element.162), channel_id=1, source_target_pairs={{0,16},{16,32},{32,48},{48,64},{64,80},{80,96},{96,112},{112,128},... | collective-permute-start | bytes 786440 | tf_op jit(solution)/shard_map/while/body/eval_jaxpr/ppermute | solution.py:10
  207.3 14.1 %collective-permute-start = (f32[256,256]{1,0:T(8,128)S(1)}, f32[256,256]{1,0:T(8,128)S(1)}, u32[]{:S(2)}, u32[]{:S(2)}) collective-permute-start(f32[256,256]{1,0:T(8,128)S(1)} %get-tuple-element.162), channel_id=1, source_target_pairs={{0,16},{16,32},{32,48},{48,64},{64,80},{80,96},{96,112},{112,128},... | collective-permute-start | bytes 786440 | tf_op jit(solution)/shard_map/while/body/eval_jaxpr/ppermute | solution.py:10
  221.3 13.5 %collective-permute-start = (f32[256,256]{1,0:T(8,128)S(1)}, f32[256,256]{1,0:T(8,128)S(1)}, u32[]{:S(2)}, u32[]{:S(2)}) collective-permute-start(f32[256,256]{1,0:T(8,128)S(1)} %get-tuple-element.162), channel_id=1, source_target_pairs={{0,16},{16,32},{32,48},{48,64},{64,80},{80,96},{96,112},{112,128},... | collective-permute-start | bytes 786440 | tf_op jit(solution)/shard_map/while/body/eval_jaxpr/ppermute | solution.py:10
  234.9 12.7 %collective-permute-start = (f32[256,256]{1,0:T(8,128)S(1)}, f32[256,256]{1,0:T(8,128)S(1)}, u32[]{:S(2)}, u32[]{:S(2)}) collective-permute-start(f32[256,256]{1,0:T(8,128)S(1)} %get-tuple-element.162), channel_id=1, source_target_pairs={{0,16},{16,32},{32,48},{48,64},{64,80},{80,96},{96,112},{112,128},... | collective-permute-start | bytes 786440 | tf_op jit(solution)/shard_map/while/body/eval_jaxpr/ppermute | solution.py:10
  247.6 11.8 %collective-permute-start = (f32[256,256]{1,0:T(8,128)S(1)}, f32[256,256]{1,0:T(8,128)S(1)}, u32[]{:S(2)}, u32[]{:S(2)}) collective-permute-start(f32[256,256]{1,0:T(8,128)S(1)} %get-tuple-element.162), channel_id=1, source_target_pairs={{0,16},{16,32},{32,48},{48,64},{64,80},{80,96},{96,112},{112,128},... | collective-permute-start | bytes 786440 | tf_op jit(solution)/shard_map/while/body/eval_jaxpr/ppermute | solution.py:10
  259.4 11.6 %collective-permute-start = (f32[256,256]{1,0:T(8,128)S(1)}, f32[256,256]{1,0:T(8,128)S(1)}, u32[]{:S(2)}, u32[]{:S(2)}) collective-permute-start(f32[256,256]{1,0:T(8,128)S(1)} %get-tuple-element.162), channel_id=1, source_target_pairs={{0,16},{16,32},{32,48},{48,64},{64,80},{80,96},{96,112},{112,128},... | collective-permute-start | bytes 786440 | tf_op jit(solution)/shard_map/while/body/eval_jaxpr/ppermute | solution.py:10
  271.0 11.6 %collective-permute-start = (f32[256,256]{1,0:T(8,128)S(1)}, f32[256,256]{1,0:T(8,128)S(1)}, u32[]{:S(2)}, u32[]{:S(2)}) collective-permute-start(f32[256,256]{1,0:T(8,128)S(1)} %get-tuple-element.162), channel_id=1, source_target_pairs={{0,16},{16,32},{32,48},{48,64},{64,80},{80,96},{96,112},{112,128},... | collective-permute-start | bytes 786440 | tf_op jit(solution)/shard_map/while/body/eval_jaxpr/ppermute | solution.py:10
  282.5 11.6 %collective-permute-start = (f32[256,256]{1,0:T(8,128)S(1)}, f32[256,256]{1,0:T(8,128)S(1)}, u32[]{:S(2)}, u32[]{:S(2)}) collective-permute-start(f32[256,256]{1,0:T(8,128)S(1)} %get-tuple-element.162), channel_id=1, source_target_pairs={{0,16},{16,32},{32,48},{48,64},{64,80},{80,96},{96,112},{112,128},... | collective-permute-start | bytes 786440 | tf_op jit(solution)/shard_map/while/body/eval_jaxpr/ppermute | solution.py:10
  294.9 11.6 %collective-permute-start = (f32[256,256]{1,0:T(8,128)S(1)}, f32[256,256]{1,0:T(8,128)S(1)}, u32[]{:S(2)}, u32[]{:S(2)}) collective-permute-start(f32[256,256]{1,0:T(8,128)S(1)} %get-tuple-element.162), channel_id=1, source_target_pairs={{0,16},{16,32},{32,48},{48,64},{64,80},{80,96},{96,112},{112,128},... | collective-permute-start | bytes 786440 | tf_op jit(solution)/shard_map/while/body/eval_jaxpr/ppermute | solution.py:10
  306.5 12.0 %collective-permute-start = (f32[256,256]{1,0:T(8,128)S(1)}, f32[256,256]{1,0:T(8,128)S(1)}, u32[]{:S(2)}, u32[]{:S(2)}) collective-permute-start(f32[256,256]{1,0:T(8,128)S(1)} %get-tuple-element.162), channel_id=1, source_target_pairs={{0,16},{16,32},{32,48},{48,64},{64,80},{80,96},{96,112},{112,128},... | collective-permute-start | bytes 786440 | tf_op jit(solution)/shard_map/while/body/eval_jaxpr/ppermute | solution.py:10
  318.5 13.1 %collective-permute-start = (f32[256,256]{1,0:T(8,128)S(1)}, f32[256,256]{1,0:T(8,128)S(1)}, u32[]{:S(2)}, u32[]{:S(2)}) collective-permute-start(f32[256,256]{1,0:T(8,128)S(1)} %get-tuple-element.162), channel_id=1, source_target_pairs={{0,16},{16,32},{32,48},{48,64},{64,80},{80,96},{96,112},{112,128},... | collective-permute-start | bytes 786440 | tf_op jit(solution)/shard_map/while/body/eval_jaxpr/ppermute | solution.py:10
  331.6 14.3 %collective-permute-start = (f32[256,256]{1,0:T(8,128)S(1)}, f32[256,256]{1,0:T(8,128)S(1)}, u32[]{:S(2)}, u32[]{:S(2)}) collective-permute-start(f32[256,256]{1,0:T(8,128)S(1)} %get-tuple-element.162), channel_id=1, source_target_pairs={{0,16},{16,32},{32,48},{48,64},{64,80},{80,96},{96,112},{112,128},... | collective-permute-start | bytes 786440 | tf_op jit(solution)/shard_map/while/body/eval_jaxpr/ppermute | solution.py:10
  345.9 13.5 %collective-permute-start = (f32[256,256]{1,0:T(8,128)S(1)}, f32[256,256]{1,0:T(8,128)S(1)}, u32[]{:S(2)}, u32[]{:S(2)}) collective-permute-start(f32[256,256]{1,0:T(8,128)S(1)} %get-tuple-element.162), channel_id=1, source_target_pairs={{0,16},{16,32},{32,48},{48,64},{64,80},{80,96},{96,112},{112,128},... | collective-permute-start | bytes 786440 | tf_op jit(solution)/shard_map/while/body/eval_jaxpr/ppermute | solution.py:10
  359.4 12.7 %collective-permute-start = (f32[256,256]{1,0:T(8,128)S(1)}, f32[256,256]{1,0:T(8,128)S(1)}, u32[]{:S(2)}, u32[]{:S(2)}) collective-permute-start(f32[256,256]{1,0:T(8,128)S(1)} %get-tuple-element.162), channel_id=1, source_target_pairs={{0,16},{16,32},{32,48},{48,64},{64,80},{80,96},{96,112},{112,128},... | collective-permute-start | bytes 786440 | tf_op jit(solution)/shard_map/while/body/eval_jaxpr/ppermute | solution.py:10
  372.1 11.8 %collective-permute-start = (f32[256,256]{1,0:T(8,128)S(1)}, f32[256,256]{1,0:T(8,128)S(1)}, u32[]{:S(2)}, u32[]{:S(2)}) collective-permute-start(f32[256,256]{1,0:T(8,128)S(1)} %get-tuple-element.162), channel_id=1, source_target_pairs={{0,16},{16,32},{32,48},{48,64},{64,80},{80,96},{96,112},{112,128},... | collective-permute-start | bytes 786440 | tf_op jit(solution)/shard_map/while/body/eval_jaxpr/ppermute | solution.py:10
  383.9 11.6 %collective-permute-start = (f32[256,256]{1,0:T(8,128)S(1)}, f32[256,256]{1,0:T(8,128)S(1)}, u32[]{:S(2)}, u32[]{:S(2)}) collective-permute-start(f32[256,256]{1,0:T(8,128)S(1)} %get-tuple-element.162), channel_id=1, source_target_pairs={{0,16},{16,32},{32,48},{48,64},{64,80},{80,96},{96,112},{112,128},... | collective-permute-start | bytes 786440 | tf_op jit(solution)/shard_map/while/body/eval_jaxpr/ppermute | solution.py:10
  395.5 11.6 %collective-permute-start = (f32[256,256]{1,0:T(8,128)S(1)}, f32[256,256]{1,0:T(8,128)S(1)}, u32[]{:S(2)}, u32[]{:S(2)}) collective-permute-start(f32[256,256]{1,0:T(8,128)S(1)} %get-tuple-element.162), channel_id=1, source_target_pairs={{0,16},{16,32},{32,48},{48,64},{64,80},{80,96},{96,112},{112,128},... | collective-permute-start | bytes 786440 | tf_op jit(solution)/shard_map/while/body/eval_jaxpr/ppermute | solution.py:10
  407.0 11.6 %collective-permute-start = (f32[256,256]{1,0:T(8,128)S(1)}, f32[256,256]{1,0:T(8,128)S(1)}, u32[]{:S(2)}, u32[]{:S(2)}) collective-permute-start(f32[256,256]{1,0:T(8,128)S(1)} %get-tuple-element.162), channel_id=1, source_target_pairs={{0,16},{16,32},{32,48},{48,64},{64,80},{80,96},{96,112},{112,128},... | collective-permute-start | bytes 786440 | tf_op jit(solution)/shard_map/while/body/eval_jaxpr/ppermute | solution.py:10
  418.6 11.6 %collective-permute-start = (f32[256,256]{1,0:T(8,128)S(1)}, f32[256,256]{1,0:T(8,128)S(1)}, u32[]{:S(2)}, u32[]{:S(2)}) collective-permute-start(f32[256,256]{1,0:T(8,128)S(1)} %get-tuple-element.162), channel_id=1, source_target_pairs={{0,16},{16,32},{32,48},{48,64},{64,80},{80,96},{96,112},{112,128},... | collective-permute-start | bytes 786440 | tf_op jit(solution)/shard_map/while/body/eval_jaxpr/ppermute | solution.py:10
  430.2 12.0 %collective-permute-start = (f32[256,256]{1,0:T(8,128)S(1)}, f32[256,256]{1,0:T(8,128)S(1)}, u32[]{:S(2)}, u32[]{:S(2)}) collective-permute-start(f32[256,256]{1,0:T(8,128)S(1)} %get-tuple-element.162), channel_id=1, source_target_pairs={{0,16},{16,32},{32,48},{48,64},{64,80},{80,96},{96,112},{112,128},... | collective-permute-start | bytes 786440 | tf_op jit(solution)/shard_map/while/body/eval_jaxpr/ppermute | solution.py:10
  442.2 11.6 %collective-permute-start = (f32[256,256]{1,0:T(8,128)S(1)}, f32[256,256]{1,0:T(8,128)S(1)}, u32[]{:S(2)}, u32[]{:S(2)}) collective-permute-start(f32[256,256]{1,0:T(8,128)S(1)} %get-tuple-element.162), channel_id=1, source_target_pairs={{0,16},{16,32},{32,48},{48,64},{64,80},{80,96},{96,112},{112,128},... | collective-permute-start | bytes 786440 | tf_op jit(solution)/shard_map/while/body/eval_jaxpr/ppermute | solution.py:10
  453.8 11.6 %collective-permute-start = (f32[256,256]{1,0:T(8,128)S(1)}, f32[256,256]{1,0:T(8,128)S(1)}, u32[]{:S(2)}, u32[]{:S(2)}) collective-permute-start(f32[256,256]{1,0:T(8,128)S(1)} %get-tuple-element.162), channel_id=1, source_target_pairs={{0,16},{16,32},{32,48},{48,64},{64,80},{80,96},{96,112},{112,128},... | collective-permute-start | bytes 786440 | tf_op jit(solution)/shard_map/while/body/eval_jaxpr/ppermute | solution.py:10
  465.4 11.6 %collective-permute-start = (f32[256,256]{1,0:T(8,128)S(1)}, f32[256,256]{1,0:T(8,128)S(1)}, u32[]{:S(2)}, u32[]{:S(2)}) collective-permute-start(f32[256,256]{1,0:T(8,128)S(1)} %get-tuple-element.162), channel_id=1, source_target_pairs={{0,16},{16,32},{32,48},{48,64},{64,80},{80,96},{96,112},{112,128},... | collective-permute-start | bytes 786440 | tf_op jit(solution)/shard_map/while/body/eval_jaxpr/ppermute | solution.py:10
  476.9 0.7 copy-start.1
Sparse Core Ops, SparseCore 0:
  10.9 46.2 all-gather.1
where the time goes:
time: 486 us; the launch traced here: 484 us
  waiting for transfers between devices  364 us (75%)
  starting transfers between devices  60.7 us (12%)
  blocking collectives  33.1 us (7%)
  between operations  14.1 us (3%)
  matrix products  10.7 us (2%)
    ppermute x31, waiting for transfers between devices, passed_along(): return lax.ppermute(x, axis, pairs)  317 us
    ppermute x31, starting transfers between devices, passed_along(): return lax.ppermute(x, axis, pairs)  60.6 us
    all_gather x1, waiting for transfers between devices, body(): lax.all_gather(picked_one, 'blk', axis=0, tiled=True)  46.4 us
    all_gather x1, blocking collectives, body(): lax.all_gather(picked_two, 'blk', axis=0, tiled=True)  18 us
    all_gather x1, blocking collectives, body(): lax.all_gather(edge_rows, 'blk', axis=0, tiled=True).astype(jnp.float32)  15.1 us
  transfers between devices with their start and end apart: 32, of which 32 were waited for; matrix products, arithmetic and copies ran while one was open for 0% of the time, Pallas kernels for 0%

commit v1 on v0

--- a/solution.py
+++ b/solution.py
@@ -41,7 +41,9 @@
         strip_block[:, panel_width:].astype(jnp.float32)
         - jnp.dot(
             columns,
-            lax.all_gather(picked_one, "blk", axis=0, tiled=True),
+            jnp.concatenate(
+                lax.all_to_all(jnp.stack([picked_one] * lax.axis_size("blk")), "blk", 0, 0), axis=0
+            ),
             preferred_element_type=jnp.float32,
         )
     ).astype(jnp.bfloat16)

time: 486 us -> 463 us (0.953)
  waiting for transfers between devices: 364 us -> 344 us
  between operations: 14.1 us -> 0.68 us
  starting transfers between devices: 60.7 us -> 71.1 us
    all_gather x1 -> x0, waiting for transfers between devices: 46.4 us -> none  [body(): lax.all_gather(picked_one, 'blk', axis=0, tiled=True)]
    all_to_all x0 -> x1, waiting for transfers between devices: none -> 26.7 us  [body(): lax.all_to_all(jnp.stack([picked_one] * lax.axis_size('blk')), 'blk', 0, 0)]
    all_to_all x0 -> x1, starting transfers between devices: none -> 10.4 us  [body(): lax.all_to_all(jnp.stack([picked_one] * lax.axis_size('blk')), 'blk', 0, 0)]
where the time goes in v1:
time: 463 us; the launch traced here: 462 us
  waiting for transfers between devices  344 us (74%)
  starting transfers between devices  71.1 us (15%)
  blocking collectives  33.6 us (7%)
  matrix products  9.74 us (2%)
    ppermute x31, waiting for transfers between devices, passed_along(): return lax.ppermute(x, axis, pairs)  317 us
    ppermute x31, starting transfers between devices, passed_along(): return lax.ppermute(x, axis, pairs)  60.7 us
    all_to_all x1, waiting for transfers between devices, body(): lax.all_to_all(jnp.stack([picked_one] * lax.axis_size('blk')), 'blk', 0, 0)  26.7 us
    all_gather x1, blocking collectives, body(): lax.all_gather(picked_two, 'blk', axis=0, tiled=True)  18.3 us
    all_gather x1, blocking collectives, body(): lax.all_gather(edge_rows, 'blk', axis=0, tiled=True).astype(jnp.float32)  15.3 us
    all_to_all x1, starting transfers between devices, body(): lax.all_to_all(jnp.stack([picked_one] * lax.axis_size('blk')), 'blk', 0, 0)  10.4 us
  transfers between devices with their start and end apart: 32, of which 32 were waited for; matrix products, arithmetic and copies ran while one was open for 0% of the time, Pallas kernels for 0%

profile of v1, /device:TPU:32, one launch (start us, length us, event | category | flops | bytes accessed | tf_op | source)
XLA Modules:
  0.0 462.3 jit_solution(17182475341930651778)
XLA Ops:
  1.5 2.0 convolution_convert_fusion.1
  4.6 10.4 %all-to-all-start = ((bf16[16,16,2048]{2,1,0:T(8,128)(2,1)}), bf16[16,16,2048]{2,1,0:T(8,128)(2,1)S(1)}, u32[]{:S(2)}, u32[]{:S(2)}) async-start(bf16[16,16,2048]{2,1,0:T(8,128)(2,1)} %stack.2), calls=%async_computation | async-start | bytes 2097152 | tf_op jit(solution)/shard_map/all_to_all | solution.py:45
  15.0 26.7 %all-to-all-done = bf16[16,16,2048]{2,1,0:T(8,128)(2,1)S(1)} async-done(((bf16[16,16,2048]{2,1,0:T(8,128)(2,1)}), bf16[16,16,2048]{2,1,0:T(8,128)(2,1)S(1)}, u32[]{:S(2)}, u32[]{:S(2)}) %all-to-all-start) | async-done | bytes 1048608 | tf_op jit(solution)/shard_map/all_to_all | solution.py:45
  41.6 2.5 subtract_convert_fusion
  44.5 18.3 %all_gather.6 = bf16[256,1792]{1,0:T(8,128)(2,1)S(1)} all-gather(bf16[16,1792]{1,0:T(8,128)(2,1)S(1)} %convolution_convert_fusion), channel_id=1, replica_groups=mesh['tm'=32,'blk'=16] {'blk'}, dimensions={0}, use_global_device_ids=true | all-gather | bytes 974848 | tf_op jit(solution)/shard_map/all_gather | solution.py:61
  62.9 3.0 subtract_convert_fusion.1
  66.9 15.3 %all_gather.7 = bf16[256,256]{1,0:T(8,128)(2,1)S(1)} all-gather(bf16[16,256]{1,0:T(8,128)(2,1)S(1)} %convolution_convert_fusion.4), channel_id=1, replica_groups=mesh['tm'=32,'blk'=16] {'blk'}, dimensions={0}, use_global_device_ids=true | all-gather | bytes 139264 | tf_op jit(solution)/shard_map/all_gather | solution.py:68
  82.3 379.3 %while.16 = (s32[]{:T(128)}, f32[256,256]{1,0:T(8,128)S(1)}, s32[]{:T(128)}, f32[256,256]{1,0:T(8,128)S(1)}, f32[256,256]{1,0:T(8,128)S(1)}, /*index=5*/s32[]{:T(128)}) while((s32[]{:T(128)}, f32[256,256]{1,0:T(8,128)S(1)}, s32[]{:T(128)}, f32[256,256]{1,0:T(8,128)S(1)}, f32[256,256]{1,0:T(8,128)S(1)}, /*index=5*/s32[]{:T(128)}) %tuple.49), condition=%wide.region_3.0_spmd, body=%wide.region_0.0_spmd.sunk | while | flops 402718720 | bytes 2883739 | solution.py:84
  82.3 3.4 collective-permute-start
  85.7 10.4 %collective-permute-done = f32[256,256]{1,0:T(8,128)S(1)} collective-permute-done((f32[256,256]{1,0:T(8,128)S(1)}, f32[256,256]{1,0:T(8,128)S(1)}, u32[]{:S(2)}, u32[]{:S(2)}) %collective-permute-start) | collective-permute-done | bytes 262176 | tf_op jit(solution)/shard_map/while/body/eval_jaxpr/ppermute | solution.py:10
  96.0 1.9 collective-permute-start
  98.0 11.0 %collective-permute-done = f32[256,256]{1,0:T(8,128)S(1)} collective-permute-done((f32[256,256]{1,0:T(8,128)S(1)}, f32[256,256]{1,0:T(8,128)S(1)}, u32[]{:S(2)}, u32[]{:S(2)}) %collective-permute-start) | collective-permute-done | bytes 262176 | tf_op jit(solution)/shard_map/while/body/eval_jaxpr/ppermute | solution.py:10
  109.0 1.9 collective-permute-start
  110.9 10.1 %collective-permute-done = f32[256,256]{1,0:T(8,128)S(1)} collective-permute-done((f32[256,256]{1,0:T(8,128)S(1)}, f32[256,256]{1,0:T(8,128)S(1)}, u32[]{:S(2)}, u32[]{:S(2)}) %collective-permute-start) | collective-permute-done | bytes 262176 | tf_op jit(solution)/shard_map/while/body/eval_jaxpr/ppermute | solution.py:10
  121.0 1.9 collective-permute-start
  122.9 9.7 %collective-permute-done = f32[256,256]{1,0:T(8,128)S(1)} collective-permute-done((f32[256,256]{1,0:T(8,128)S(1)}, f32[256,256]{1,0:T(8,128)S(1)}, u32[]{:S(2)}, u32[]{:S(2)}) %collective-permute-start) | collective-permute-done | bytes 262176 | tf_op jit(solution)/shard_map/while/body/eval_jaxpr/ppermute | solution.py:10
  132.6 1.9 collective-permute-start
  134.5 9.7 %collective-permute-done = f32[256,256]{1,0:T(8,128)S(1)} collective-permute-done((f32[256,256]{1,0:T(8,128)S(1)}, f32[256,256]{1,0:T(8,128)S(1)}, u32[]{:S(2)}, u32[]{:S(2)}) %collective-permute-start) | collective-permute-done | bytes 262176 | tf_op jit(solution)/shard_map/while/body/eval_jaxpr/ppermute | solution.py:10
  144.2 1.9 collective-permute-start
  146.1 9.7 %collective-permute-done = f32[256,256]{1,0:T(8,128)S(1)} collective-permute-done((f32[256,256]{1,0:T(8,128)S(1)}, f32[256,256]{1,0:T(8,128)S(1)}, u32[]{:S(2)}, u32[]{:S(2)}) %collective-permute-start) | collective-permute-done | bytes 262176 | tf_op jit(solution)/shard_map/while/body/eval_jaxpr/ppermute | solution.py:10
  157.7 9.7 %collective-permute-done = f32[256,256]{1,0:T(8,128)S(1)} collective-permute-done((f32[256,256]{1,0:T(8,128)S(1)}, f32[256,256]{1,0:T(8,128)S(1)}, u32[]{:S(2)}, u32[]{:S(2)}) %collective-permute-start) | collective-permute-done | bytes 262176 | tf_op jit(solution)/shard_map/while/body/eval_jaxpr/ppermute | solution.py:10
  167.3 1.9 collective-permute-start
  169.2 9.8 %collective-permute-done = f32[256,256]{1,0:T(8,128)S(1)} collective-permute-done((f32[256,256]{1,0:T(8,128)S(1)}, f32[256,256]{1,0:T(8,128)S(1)}, u32[]{:S(2)}, u32[]{:S(2)}) %collective-permute-start) | collective-permute-done | bytes 262176 | tf_op jit(solution)/shard_map/while/body/eval_jaxpr/ppermute | solution.py:10
  181.0 10.9 %collective-permute-done = f32[256,256]{1,0:T(8,128)S(1)} collective-permute-done((f32[256,256]{1,0:T(8,128)S(1)}, f32[256,256]{1,0:T(8,128)S(1)}, u32[]{:S(2)}, u32[]{:S(2)}) %collective-permute-start) | collective-permute-done | bytes 262176 | tf_op jit(solution)/shard_map/while/body/eval_jaxpr/ppermute | solution.py:10
  193.8 12.1 %collective-permute-done = f32[256,256]{1,0:T(8,128)S(1)} collective-permute-done((f32[256,256]{1,0:T(8,128)S(1)}, f32[256,256]{1,0:T(8,128)S(1)}, u32[]{:S(2)}, u32[]{:S(2)}) %collective-permute-start) | collective-permute-done | bytes 262176 | tf_op jit(solution)/shard_map/while/body/eval_jaxpr/ppermute | solution.py:10
  207.9 11.6 %collective-permute-done = f32[256,256]{1,0:T(8,128)S(1)} collective-permute-done((f32[256,256]{1,0:T(8,128)S(1)}, f32[256,256]{1,0:T(8,128)S(1)}, u32[]{:S(2)}, u32[]{:S(2)}) %collective-permute-start) | collective-permute-done | bytes 262176 | tf_op jit(solution)/shard_map/while/body/eval_jaxpr/ppermute | solution.py:10
  221.5 10.8 %collective-permute-done = f32[256,256]{1,0:T(8,128)S(1)} collective-permute-done((f32[256,256]{1,0:T(8,128)S(1)}, f32[256,256]{1,0:T(8,128)S(1)}, u32[]{:S(2)}, u32[]{:S(2)}) %collective-permute-start) | collective-permute-done | bytes 262176 | tf_op jit(solution)/shard_map/while/body/eval_jaxpr/ppermute | solution.py:10
  232.3 1.9 collective-permute-start
  234.2 9.9 %collective-permute-done = f32[256,256]{1,0:T(8,128)S(1)} collective-permute-done((f32[256,256]{1,0:T(8,128)S(1)}, f32[256,256]{1,0:T(8,128)S(1)}, u32[]{:S(2)}, u32[]{:S(2)}) %collective-permute-start) | collective-permute-done | bytes 262176 | tf_op jit(solution)/shard_map/while/body/eval_jaxpr/ppermute | solution.py:10
  246.0 9.7 %collective-permute-done = f32[256,256]{1,0:T(8,128)S(1)} collective-permute-done((f32[256,256]{1,0:T(8,128)S(1)}, f32[256,256]{1,0:T(8,128)S(1)}, u32[]{:S(2)}, u32[]{:S(2)}) %collective-permute-start) | collective-permute-done | bytes 262176 | tf_op jit(solution)/shard_map/while/body/eval_jaxpr/ppermute | solution.py:10
  257.5 9.7 %collective-permute-done = f32[256,256]{1,0:T(8,128)S(1)} collective-permute-done((f32[256,256]{1,0:T(8,128)S(1)}, f32[256,256]{1,0:T(8,128)S(1)}, u32[]{:S(2)}, u32[]{:S(2)}) %collective-permute-start) | collective-permute-done | bytes 262176 | tf_op jit(solution)/shard_map/while/body/eval_jaxpr/ppermute | solution.py:10
  269.1 9.7 %collective-permute-done = f32[256,256]{1,0:T(8,128)S(1)} collective-permute-done((f32[256,256]{1,0:T(8,128)S(1)}, f32[256,256]{1,0:T(8,128)S(1)}, u32[]{:S(2)}, u32[]{:S(2)}) %collective-permute-start) | collective-permute-done | bytes 262176 | tf_op jit(solution)/shard_map/while/body/eval_jaxpr/ppermute | solution.py:10
  279.6 1.9 collective-permute-start
  281.5 9.7 %collective-permute-done = f32[256,256]{1,0:T(8,128)S(1)} collective-permute-done((f32[256,256]{1,0:T(8,128)S(1)}, f32[256,256]{1,0:T(8,128)S(1)}, u32[]{:S(2)}, u32[]{:S(2)}) %collective-permute-start) | collective-permute-done | bytes 262176 | tf_op jit(solution)/shard_map/while/body/eval_jaxpr/ppermute | solution.py:10
  293.1 10.1 %collective-permute-done = f32[256,256]{1,0:T(8,128)S(1)} collective-permute-done((f32[256,256]{1,0:T(8,128)S(1)}, f32[256,256]{1,0:T(8,128)S(1)}, u32[]{:S(2)}, u32[]{:S(2)}) %collective-permute-start) | collective-permute-done | bytes 262176 | tf_op jit(solution)/shard_map/while/body/eval_jaxpr/ppermute | solution.py:10
  305.1 11.2 %collective-permute-done = f32[256,256]{1,0:T(8,128)S(1)} collective-permute-done((f32[256,256]{1,0:T(8,128)S(1)}, f32[256,256]{1,0:T(8,128)S(1)}, u32[]{:S(2)}, u32[]{:S(2)}) %collective-permute-start) | collective-permute-done | bytes 262176 | tf_op jit(solution)/shard_map/while/body/eval_jaxpr/ppermute | solution.py:10
  318.2 12.3 %collective-permute-done = f32[256,256]{1,0:T(8,128)S(1)} collective-permute-done((f32[256,256]{1,0:T(8,128)S(1)}, f32[256,256]{1,0:T(8,128)S(1)}, u32[]{:S(2)}, u32[]{:S(2)}) %collective-permute-start) | collective-permute-done | bytes 262176 | tf_op jit(solution)/shard_map/while/body/eval_jaxpr/ppermute | solution.py:10
  332.5 11.6 %collective-permute-done = f32[256,256]{1,0:T(8,128)S(1)} collective-permute-done((f32[256,256]{1,0:T(8,128)S(1)}, f32[256,256]{1,0:T(8,128)S(1)}, u32[]{:S(2)}, u32[]{:S(2)}) %collective-permute-start) | collective-permute-done | bytes 262176 | tf_op jit(solution)/shard_map/while/body/eval_jaxpr/ppermute | solution.py:10
  346.0 10.8 %collective-permute-done = f32[256,256]{1,0:T(8,128)S(1)} collective-permute-done((f32[256,256]{1,0:T(8,128)S(1)}, f32[256,256]{1,0:T(8,128)S(1)}, u32[]{:S(2)}, u32[]{:S(2)}) %collective-permute-start) | collective-permute-done | bytes 262176 | tf_op jit(solution)/shard_map/while/body/eval_jaxpr/ppermute | solution.py:10
  358.7 9.8 %collective-permute-done = f32[256,256]{1,0:T(8,128)S(1)} collective-permute-done((f32[256,256]{1,0:T(8,128)S(1)}, f32[256,256]{1,0:T(8,128)S(1)}, u32[]{:S(2)}, u32[]{:S(2)}) %collective-permute-start) | collective-permute-done | bytes 262176 | tf_op jit(solution)/shard_map/while/body/eval_jaxpr/ppermute | solution.py:10
  370.5 9.7 %collective-permute-done = f32[256,256]{1,0:T(8,128)S(1)} collective-permute-done((f32[256,256]{1,0:T(8,128)S(1)}, f32[256,256]{1,0:T(8,128)S(1)}, u32[]{:S(2)}, u32[]{:S(2)}) %collective-permute-start) | collective-permute-done | bytes 262176 | tf_op jit(solution)/shard_map/while/body/eval_jaxpr/ppermute | solution.py:10
  382.0 9.7 %collective-permute-done = f32[256,256]{1,0:T(8,128)S(1)} collective-permute-done((f32[256,256]{1,0:T(8,128)S(1)}, f32[256,256]{1,0:T(8,128)S(1)}, u32[]{:S(2)}, u32[]{:S(2)}) %collective-permute-start) | collective-permute-done | bytes 262176 | tf_op jit(solution)/shard_map/while/body/eval_jaxpr/ppermute | solution.py:10
  393.6 9.7 %collective-permute-done = f32[256,256]{1,0:T(8,128)S(1)} collective-permute-done((f32[256,256]{1,0:T(8,128)S(1)}, f32[256,256]{1,0:T(8,128)S(1)}, u32[]{:S(2)}, u32[]{:S(2)}) %collective-permute-start) | collective-permute-done | bytes 262176 | tf_op jit(solution)/shard_map/while/body/eval_jaxpr/ppermute | solution.py:10
  405.2 9.7 %collective-permute-done = f32[256,256]{1,0:T(8,128)S(1)} collective-permute-done((f32[256,256]{1,0:T(8,128)S(1)}, f32[256,256]{1,0:T(8,128)S(1)}, u32[]{:S(2)}, u32[]{:S(2)}) %collective-permute-start) | collective-permute-done | bytes 262176 | tf_op jit(solution)/shard_map/while/body/eval_jaxpr/ppermute | solution.py:10
  416.8 10.1 %collective-permute-done = f32[256,256]{1,0:T(8,128)S(1)} collective-permute-done((f32[256,256]{1,0:T(8,128)S(1)}, f32[256,256]{1,0:T(8,128)S(1)}, u32[]{:S(2)}, u32[]{:S(2)}) %collective-permute-start) | collective-permute-done | bytes 262176 | tf_op jit(solution)/shard_map/while/body/eval_jaxpr/ppermute | solution.py:10
  428.8 9.7 %collective-permute-done = f32[256,256]{1,0:T(8,128)S(1)} collective-permute-done((f32[256,256]{1,0:T(8,128)S(1)}, f32[256,256]{1,0:T(8,128)S(1)}, u32[]{:S(2)}, u32[]{:S(2)}) %collective-permute-start) | collective-permute-done | bytes 262176 | tf_op jit(solution)/shard_map/while/body/eval_jaxpr/ppermute | solution.py:10
  440.4 9.7 %collective-permute-done = f32[256,256]{1,0:T(8,128)S(1)} collective-permute-done((f32[256,256]{1,0:T(8,128)S(1)}, f32[256,256]{1,0:T(8,128)S(1)}, u32[]{:S(2)}, u32[]{:S(2)}) %collective-permute-start) | collective-permute-done | bytes 262176 | tf_op jit(solution)/shard_map/while/body/eval_jaxpr/ppermute | solution.py:10
  451.9 9.7 %collective-permute-done = f32[256,256]{1,0:T(8,128)S(1)} collective-permute-done((f32[256,256]{1,0:T(8,128)S(1)}, f32[256,256]{1,0:T(8,128)S(1)}, u32[]{:S(2)}, u32[]{:S(2)}) %collective-permute-start) | collective-permute-done | bytes 262176 | tf_op jit(solution)/shard_map/while/body/eval_jaxpr/ppermute | solution.py:10
  (68 shorter events, 47.7 us)
Async XLA Ops:
  3.5 38.2 %copy-start.2 = (bf16[1,2,256,256]{3,2,1,0:T(8,128)(2,1)S(1)}, bf16[1,2,256,256]{3,2,1,0:T(8,128)(2,1)}, u32[]{:S(2)}) copy-start(bf16[1,2,256,256]{3,2,1,0:T(8,128)(2,1)} %param.9) | copy-start | bytes 786436
  4.6 37.1 %all-to-all-start = ((bf16[16,16,2048]{2,1,0:T(8,128)(2,1)}), bf16[16,16,2048]{2,1,0:T(8,128)(2,1)S(1)}, u32[]{:S(2)}, u32[]{:S(2)}) async-start(bf16[16,16,2048]{2,1,0:T(8,128)(2,1)} %stack.2), calls=%async_computation | async-start | bytes 2097152 | tf_op jit(solution)/shard_map/all_to_all | solution.py:45
  62.8 19.4 %copy-start = (f32[1,256,256]{2,1,0:T(8,128)S(1)}, f32[1,256,256]{2,1,0:T(8,128)}, u32[]{:S(2)}) copy-start(f32[1,256,256]{2,1,0:T(8,128)} %param.10) | copy-start | bytes 786436
  82.3 13.8 %collective-permute-start = (f32[256,256]{1,0:T(8,128)S(1)}, f32[256,256]{1,0:T(8,128)S(1)}, u32[]{:S(2)}, u32[]{:S(2)}) collective-permute-start(f32[256,256]{1,0:T(8,128)S(1)} %get-tuple-element.162), channel_id=1, source_target_pairs={{0,16},{16,32},{32,48},{48,64},{64,80},{80,96},{96,112},{112,128},... | collective-permute-start | bytes 786440 | tf_op jit(solution)/shard_map/while/body/eval_jaxpr/ppermute | solution.py:10
  96.0 13.0 %collective-permute-start = (f32[256,256]{1,0:T(8,128)S(1)}, f32[256,256]{1,0:T(8,128)S(1)}, u32[]{:S(2)}, u32[]{:S(2)}) collective-permute-start(f32[256,256]{1,0:T(8,128)S(1)} %get-tuple-element.162), channel_id=1, source_target_pairs={{0,16},{16,32},{32,48},{48,64},{64,80},{80,96},{96,112},{112,128},... | collective-permute-start | bytes 786440 | tf_op jit(solution)/shard_map/while/body/eval_jaxpr/ppermute | solution.py:10
  109.0 12.0 %collective-permute-start = (f32[256,256]{1,0:T(8,128)S(1)}, f32[256,256]{1,0:T(8,128)S(1)}, u32[]{:S(2)}, u32[]{:S(2)}) collective-permute-start(f32[256,256]{1,0:T(8,128)S(1)} %get-tuple-element.162), channel_id=1, source_target_pairs={{0,16},{16,32},{32,48},{48,64},{64,80},{80,96},{96,112},{112,128},... | collective-permute-start | bytes 786440 | tf_op jit(solution)/shard_map/while/body/eval_jaxpr/ppermute | solution.py:10
  121.0 11.6 %collective-permute-start = (f32[256,256]{1,0:T(8,128)S(1)}, f32[256,256]{1,0:T(8,128)S(1)}, u32[]{:S(2)}, u32[]{:S(2)}) collective-permute-start(f32[256,256]{1,0:T(8,128)S(1)} %get-tuple-element.162), channel_id=1, source_target_pairs={{0,16},{16,32},{32,48},{48,64},{64,80},{80,96},{96,112},{112,128},... | collective-permute-start | bytes 786440 | tf_op jit(solution)/shard_map/while/body/eval_jaxpr/ppermute | solution.py:10
  132.6 11.6 %collective-permute-start = (f32[256,256]{1,0:T(8,128)S(1)}, f32[256,256]{1,0:T(8,128)S(1)}, u32[]{:S(2)}, u32[]{:S(2)}) collective-permute-start(f32[256,256]{1,0:T(8,128)S(1)} %get-tuple-element.162), channel_id=1, source_target_pairs={{0,16},{16,32},{32,48},{48,64},{64,80},{80,96},{96,112},{112,128},... | collective-permute-start | bytes 786440 | tf_op jit(solution)/shard_map/while/body/eval_jaxpr/ppermute | solution.py:10
  144.2 11.6 %collective-permute-start = (f32[256,256]{1,0:T(8,128)S(1)}, f32[256,256]{1,0:T(8,128)S(1)}, u32[]{:S(2)}, u32[]{:S(2)}) collective-permute-start(f32[256,256]{1,0:T(8,128)S(1)} %get-tuple-element.162), channel_id=1, source_target_pairs={{0,16},{16,32},{32,48},{48,64},{64,80},{80,96},{96,112},{112,128},... | collective-permute-start | bytes 786440 | tf_op jit(solution)/shard_map/while/body/eval_jaxpr/ppermute | solution.py:10
  155.7 11.6 %collective-permute-start = (f32[256,256]{1,0:T(8,128)S(1)}, f32[256,256]{1,0:T(8,128)S(1)}, u32[]{:S(2)}, u32[]{:S(2)}) collective-permute-start(f32[256,256]{1,0:T(8,128)S(1)} %get-tuple-element.162), channel_id=1, source_target_pairs={{0,16},{16,32},{32,48},{48,64},{64,80},{80,96},{96,112},{112,128},... | collective-permute-start | bytes 786440 | tf_op jit(solution)/shard_map/while/body/eval_jaxpr/ppermute | solution.py:10
  167.3 11.8 %collective-permute-start = (f32[256,256]{1,0:T(8,128)S(1)}, f32[256,256]{1,0:T(8,128)S(1)}, u32[]{:S(2)}, u32[]{:S(2)}) collective-permute-start(f32[256,256]{1,0:T(8,128)S(1)} %get-tuple-element.162), channel_id=1, source_target_pairs={{0,16},{16,32},{32,48},{48,64},{64,80},{80,96},{96,112},{112,128},... | collective-permute-start | bytes 786440 | tf_op jit(solution)/shard_map/while/body/eval_jaxpr/ppermute | solution.py:10
  179.1 12.8 %collective-permute-start = (f32[256,256]{1,0:T(8,128)S(1)}, f32[256,256]{1,0:T(8,128)S(1)}, u32[]{:S(2)}, u32[]{:S(2)}) collective-permute-start(f32[256,256]{1,0:T(8,128)S(1)} %get-tuple-element.162), channel_id=1, source_target_pairs={{0,16},{16,32},{32,48},{48,64},{64,80},{80,96},{96,112},{112,128},... | collective-permute-start | bytes 786440 | tf_op jit(solution)/shard_map/while/body/eval_jaxpr/ppermute | solution.py:10
  191.9 14.1 %collective-permute-start = (f32[256,256]{1,0:T(8,128)S(1)}, f32[256,256]{1,0:T(8,128)S(1)}, u32[]{:S(2)}, u32[]{:S(2)}) collective-permute-start(f32[256,256]{1,0:T(8,128)S(1)} %get-tuple-element.162), channel_id=1, source_target_pairs={{0,16},{16,32},{32,48},{48,64},{64,80},{80,96},{96,112},{112,128},... | collective-permute-start | bytes 786440 | tf_op jit(solution)/shard_map/while/body/eval_jaxpr/ppermute | solution.py:10
  206.0 13.5 %collective-permute-start = (f32[256,256]{1,0:T(8,128)S(1)}, f32[256,256]{1,0:T(8,128)S(1)}, u32[]{:S(2)}, u32[]{:S(2)}) collective-permute-start(f32[256,256]{1,0:T(8,128)S(1)} %get-tuple-element.162), channel_id=1, source_target_pairs={{0,16},{16,32},{32,48},{48,64},{64,80},{80,96},{96,112},{112,128},... | collective-permute-start | bytes 786440 | tf_op jit(solution)/shard_map/while/body/eval_jaxpr/ppermute | solution.py:10
  219.5 12.7 %collective-permute-start = (f32[256,256]{1,0:T(8,128)S(1)}, f32[256,256]{1,0:T(8,128)S(1)}, u32[]{:S(2)}, u32[]{:S(2)}) collective-permute-start(f32[256,256]{1,0:T(8,128)S(1)} %get-tuple-element.162), channel_id=1, source_target_pairs={{0,16},{16,32},{32,48},{48,64},{64,80},{80,96},{96,112},{112,128},... | collective-permute-start | bytes 786440 | tf_op jit(solution)/shard_map/while/body/eval_jaxpr/ppermute | solution.py:10
  232.3 11.8 %collective-permute-start = (f32[256,256]{1,0:T(8,128)S(1)}, f32[256,256]{1,0:T(8,128)S(1)}, u32[]{:S(2)}, u32[]{:S(2)}) collective-permute-start(f32[256,256]{1,0:T(8,128)S(1)} %get-tuple-element.162), channel_id=1, source_target_pairs={{0,16},{16,32},{32,48},{48,64},{64,80},{80,96},{96,112},{112,128},... | collective-permute-start | bytes 786440 | tf_op jit(solution)/shard_map/while/body/eval_jaxpr/ppermute | solution.py:10
  244.0 11.6 %collective-permute-start = (f32[256,256]{1,0:T(8,128)S(1)}, f32[256,256]{1,0:T(8,128)S(1)}, u32[]{:S(2)}, u32[]{:S(2)}) collective-permute-start(f32[256,256]{1,0:T(8,128)S(1)} %get-tuple-element.162), channel_id=1, source_target_pairs={{0,16},{16,32},{32,48},{48,64},{64,80},{80,96},{96,112},{112,128},... | collective-permute-start | bytes 786440 | tf_op jit(solution)/shard_map/while/body/eval_jaxpr/ppermute | solution.py:10
  255.6 11.6 %collective-permute-start = (f32[256,256]{1,0:T(8,128)S(1)}, f32[256,256]{1,0:T(8,128)S(1)}, u32[]{:S(2)}, u32[]{:S(2)}) collective-permute-start(f32[256,256]{1,0:T(8,128)S(1)} %get-tuple-element.162), channel_id=1, source_target_pairs={{0,16},{16,32},{32,48},{48,64},{64,80},{80,96},{96,112},{112,128},... | collective-permute-start | bytes 786440 | tf_op jit(solution)/shard_map/while/body/eval_jaxpr/ppermute | solution.py:10
  267.2 11.6 %collective-permute-start = (f32[256,256]{1,0:T(8,128)S(1)}, f32[256,256]{1,0:T(8,128)S(1)}, u32[]{:S(2)}, u32[]{:S(2)}) collective-permute-start(f32[256,256]{1,0:T(8,128)S(1)} %get-tuple-element.162), channel_id=1, source_target_pairs={{0,16},{16,32},{32,48},{48,64},{64,80},{80,96},{96,112},{112,128},... | collective-permute-start | bytes 786440 | tf_op jit(solution)/shard_map/while/body/eval_jaxpr/ppermute | solution.py:10
  279.6 11.6 %collective-permute-start = (f32[256,256]{1,0:T(8,128)S(1)}, f32[256,256]{1,0:T(8,128)S(1)}, u32[]{:S(2)}, u32[]{:S(2)}) collective-permute-start(f32[256,256]{1,0:T(8,128)S(1)} %get-tuple-element.162), channel_id=1, source_target_pairs={{0,16},{16,32},{32,48},{48,64},{64,80},{80,96},{96,112},{112,128},... | collective-permute-start | bytes 786440 | tf_op jit(solution)/shard_map/while/body/eval_jaxpr/ppermute | solution.py:10
  291.2 12.0 %collective-permute-start = (f32[256,256]{1,0:T(8,128)S(1)}, f32[256,256]{1,0:T(8,128)S(1)}, u32[]{:S(2)}, u32[]{:S(2)}) collective-permute-start(f32[256,256]{1,0:T(8,128)S(1)} %get-tuple-element.162), channel_id=1, source_target_pairs={{0,16},{16,32},{32,48},{48,64},{64,80},{80,96},{96,112},{112,128},... | collective-permute-start | bytes 786440 | tf_op jit(solution)/shard_map/while/body/eval_jaxpr/ppermute | solution.py:10
  303.2 13.1 %collective-permute-start = (f32[256,256]{1,0:T(8,128)S(1)}, f32[256,256]{1,0:T(8,128)S(1)}, u32[]{:S(2)}, u32[]{:S(2)}) collective-permute-start(f32[256,256]{1,0:T(8,128)S(1)} %get-tuple-element.162), channel_id=1, source_target_pairs={{0,16},{16,32},{32,48},{48,64},{64,80},{80,96},{96,112},{112,128},... | collective-permute-start | bytes 786440 | tf_op jit(solution)/shard_map/while/body/eval_jaxpr/ppermute | solution.py:10
  316.3 14.3 %collective-permute-start = (f32[256,256]{1,0:T(8,128)S(1)}, f32[256,256]{1,0:T(8,128)S(1)}, u32[]{:S(2)}, u32[]{:S(2)}) collective-permute-start(f32[256,256]{1,0:T(8,128)S(1)} %get-tuple-element.162), channel_id=1, source_target_pairs={{0,16},{16,32},{32,48},{48,64},{64,80},{80,96},{96,112},{112,128},... | collective-permute-start | bytes 786440 | tf_op jit(solution)/shard_map/while/body/eval_jaxpr/ppermute | solution.py:10
  330.5 13.5 %collective-permute-start = (f32[256,256]{1,0:T(8,128)S(1)}, f32[256,256]{1,0:T(8,128)S(1)}, u32[]{:S(2)}, u32[]{:S(2)}) collective-permute-start(f32[256,256]{1,0:T(8,128)S(1)} %get-tuple-element.162), channel_id=1, source_target_pairs={{0,16},{16,32},{32,48},{48,64},{64,80},{80,96},{96,112},{112,128},... | collective-permute-start | bytes 786440 | tf_op jit(solution)/shard_map/while/body/eval_jaxpr/ppermute | solution.py:10
  344.1 12.7 %collective-permute-start = (f32[256,256]{1,0:T(8,128)S(1)}, f32[256,256]{1,0:T(8,128)S(1)}, u32[]{:S(2)}, u32[]{:S(2)}) collective-permute-start(f32[256,256]{1,0:T(8,128)S(1)} %get-tuple-element.162), channel_id=1, source_target_pairs={{0,16},{16,32},{32,48},{48,64},{64,80},{80,96},{96,112},{112,128},... | collective-permute-start | bytes 786440 | tf_op jit(solution)/shard_map/while/body/eval_jaxpr/ppermute | solution.py:10
  356.8 11.8 %collective-permute-start = (f32[256,256]{1,0:T(8,128)S(1)}, f32[256,256]{1,0:T(8,128)S(1)}, u32[]{:S(2)}, u32[]{:S(2)}) collective-permute-start(f32[256,256]{1,0:T(8,128)S(1)} %get-tuple-element.162), channel_id=1, source_target_pairs={{0,16},{16,32},{32,48},{48,64},{64,80},{80,96},{96,112},{112,128},... | collective-permute-start | bytes 786440 | tf_op jit(solution)/shard_map/while/body/eval_jaxpr/ppermute | solution.py:10
  368.5 11.6 %collective-permute-start = (f32[256,256]{1,0:T(8,128)S(1)}, f32[256,256]{1,0:T(8,128)S(1)}, u32[]{:S(2)}, u32[]{:S(2)}) collective-permute-start(f32[256,256]{1,0:T(8,128)S(1)} %get-tuple-element.162), channel_id=1, source_target_pairs={{0,16},{16,32},{32,48},{48,64},{64,80},{80,96},{96,112},{112,128},... | collective-permute-start | bytes 786440 | tf_op jit(solution)/shard_map/while/body/eval_jaxpr/ppermute | solution.py:10
  380.1 11.6 %collective-permute-start = (f32[256,256]{1,0:T(8,128)S(1)}, f32[256,256]{1,0:T(8,128)S(1)}, u32[]{:S(2)}, u32[]{:S(2)}) collective-permute-start(f32[256,256]{1,0:T(8,128)S(1)} %get-tuple-element.162), channel_id=1, source_target_pairs={{0,16},{16,32},{32,48},{48,64},{64,80},{80,96},{96,112},{112,128},... | collective-permute-start | bytes 786440 | tf_op jit(solution)/shard_map/while/body/eval_jaxpr/ppermute | solution.py:10
  391.7 11.6 %collective-permute-start = (f32[256,256]{1,0:T(8,128)S(1)}, f32[256,256]{1,0:T(8,128)S(1)}, u32[]{:S(2)}, u32[]{:S(2)}) collective-permute-start(f32[256,256]{1,0:T(8,128)S(1)} %get-tuple-element.162), channel_id=1, source_target_pairs={{0,16},{16,32},{32,48},{48,64},{64,80},{80,96},{96,112},{112,128},... | collective-permute-start | bytes 786440 | tf_op jit(solution)/shard_map/while/body/eval_jaxpr/ppermute | solution.py:10
  403.3 11.6 %collective-permute-start = (f32[256,256]{1,0:T(8,128)S(1)}, f32[256,256]{1,0:T(8,128)S(1)}, u32[]{:S(2)}, u32[]{:S(2)}) collective-permute-start(f32[256,256]{1,0:T(8,128)S(1)} %get-tuple-element.162), channel_id=1, source_target_pairs={{0,16},{16,32},{32,48},{48,64},{64,80},{80,96},{96,112},{112,128},... | collective-permute-start | bytes 786440 | tf_op jit(solution)/shard_map/while/body/eval_jaxpr/ppermute | solution.py:10
  414.8 12.0 %collective-permute-start = (f32[256,256]{1,0:T(8,128)S(1)}, f32[256,256]{1,0:T(8,128)S(1)}, u32[]{:S(2)}, u32[]{:S(2)}) collective-permute-start(f32[256,256]{1,0:T(8,128)S(1)} %get-tuple-element.162), channel_id=1, source_target_pairs={{0,16},{16,32},{32,48},{48,64},{64,80},{80,96},{96,112},{112,128},... | collective-permute-start | bytes 786440 | tf_op jit(solution)/shard_map/while/body/eval_jaxpr/ppermute | solution.py:10
  426.9 11.6 %collective-permute-start = (f32[256,256]{1,0:T(8,128)S(1)}, f32[256,256]{1,0:T(8,128)S(1)}, u32[]{:S(2)}, u32[]{:S(2)}) collective-permute-start(f32[256,256]{1,0:T(8,128)S(1)} %get-tuple-element.162), channel_id=1, source_target_pairs={{0,16},{16,32},{32,48},{48,64},{64,80},{80,96},{96,112},{112,128},... | collective-permute-start | bytes 786440 | tf_op jit(solution)/shard_map/while/body/eval_jaxpr/ppermute | solution.py:10
  438.4 11.6 %collective-permute-start = (f32[256,256]{1,0:T(8,128)S(1)}, f32[256,256]{1,0:T(8,128)S(1)}, u32[]{:S(2)}, u32[]{:S(2)}) collective-permute-start(f32[256,256]{1,0:T(8,128)S(1)} %get-tuple-element.162), channel_id=1, source_target_pairs={{0,16},{16,32},{32,48},{48,64},{64,80},{80,96},{96,112},{112,128},... | collective-permute-start | bytes 786440 | tf_op jit(solution)/shard_map/while/body/eval_jaxpr/ppermute | solution.py:10
  450.0 11.6 %collective-permute-start = (f32[256,256]{1,0:T(8,128)S(1)}, f32[256,256]{1,0:T(8,128)S(1)}, u32[]{:S(2)}, u32[]{:S(2)}) collective-permute-start(f32[256,256]{1,0:T(8,128)S(1)} %get-tuple-element.162), channel_id=1, source_target_pairs={{0,16},{16,32},{32,48},{48,64},{64,80},{80,96},{96,112},{112,128},... | collective-permute-start | bytes 786440 | tf_op jit(solution)/shard_map/while/body/eval_jaxpr/ppermute | solution.py:10
  461.6 0.7 copy-start.1
